TPU v7x, 256 devices: a whole 4x4x8 slice. The times are simulated.
256 devices in a mesh: grp: 16 (over z, core), ep: 16 (over y, x).
Axes of the slice: x: 4, y: 4, z: 8, core: 2. Of those that a mesh axis runs over, the one named last changes fastest.
Arguments:
- queries: bfloat16 [1024, 64, 576], P(('grp', 'ep')), may hold values from -75 to 75
- cache: bfloat16 [1024, 256, 576], P(('grp', 'ep')), may hold values from -6 to 6
- lengths: int32 [1024], P(('grp', 'ep')), may hold values from 2 to 256, as said below
- live_rows: int32 [256], P(('grp', 'ep')), may hold values from 1 to 4, as said below
- tokens: bfloat16 [4096, 3584], P(('grp', 'ep')), may hold values from -6 to 6
- ids: int32 [4096, 8], P(('grp', 'ep')), may hold values from 0 to 127, all different within a row; in each aligned block of 16 rows (0 to 15, 16 to 31, ...) at most 2 rows name the same one
- gates: float32 [4096, 8], P(('grp', 'ep')), may hold values from 0.1 to 1
- w_gate: bfloat16 [256, 3584, 512], P(('grp', 'ep')), may hold values from -0.09375 to 0.09375
- w_up: bfloat16 [256, 3584, 512], P(('grp', 'ep')), may hold values from -0.09375 to 0.09375
- w_down: bfloat16 [256, 512, 3584], P(('grp', 'ep')), may hold values from -0.1875 to 0.1875
Outputs:
- context: bfloat16 [1024, 64, 512], P(('grp', 'ep'))
- mixed: bfloat16 [4096, 3584], P(('grp', 'ep'))
Inputs may be any that keep to these rules, and one draw needn't show every extreme that they name: `ids`: each row names 8 different experts; among the rows of one device no expert is named more than 2 times. `lengths`: the first request slot of every device holds 256 positions. `live_rows`: a device's live request slots are its first ones; on a quarter of the grp indices every device holds 2 or fewer, elsewhere exactly 4.
All inputs are finite; a program needn't handle non-finite values.
Results may differ from a plain program's by a relative error of at most 0.012.
Values may be sent and summed in bfloat16 or wider, within the bound.
A program may use at most 128 MiB of HBM per device.

v0:
```python
import jax
import jax.numpy as jnp
from jax import lax
from jax.sharding import PartitionSpec as P

TOPK = 8
LAT = 512
CAP = 2
score_scale = 192.0 ** (-0.5)
neg_large = -1e30


def attend(queries, cache, lengths, live_count):
    scores = (
        jnp.einsum("rhc,rlc->rhl", queries, cache, preferred_element_type=jnp.float32) * score_scale
    )
    positions = lax.broadcasted_iota(jnp.int32, scores.shape, 2)
    inside = positions < lengths[:, None, None]
    masked = jnp.where(inside, scores, neg_large)
    highest = jnp.max(masked, axis=2, keepdims=True)
    powers = jnp.where(inside, jnp.exp(masked - highest), 0.0)
    totals = jnp.sum(powers, axis=2, keepdims=True)
    weights = (powers / totals).astype(jnp.bfloat16)
    context = jnp.einsum(
        "rhl,rlc->rhc", weights, cache[:, :, :LAT], preferred_element_type=jnp.float32
    ).astype(jnp.bfloat16)
    request_slot = lax.broadcasted_iota(jnp.int32, context.shape, 0)
    return jnp.where(request_slot < live_count, context, jnp.zeros_like(context))


def expert_partial(flat_rows, w_gate, w_up, w_down):
    gate_part = jnp.dot(flat_rows, w_gate[0], preferred_element_type=jnp.float32)
    up_part = jnp.dot(flat_rows, w_up[0], preferred_element_type=jnp.float32)
    hidden = (jax.nn.silu(gate_part) * up_part).astype(jnp.bfloat16)
    return jnp.dot(hidden, w_down[0], preferred_element_type=jnp.float32)


def per_device(queries, cache, lengths, live_rows, tokens, ids, gates, w_gate, w_up, w_down):
    context = attend(queries, cache, lengths, live_rows[0])
    group_count = lax.axis_size("grp")
    peer_count = lax.axis_size("ep")
    pair_count = peer_count // 2
    row_count = tokens.shape[0]
    feature = tokens.shape[1]
    expert_slots = group_count * CAP
    slot_count = pair_count * expert_slots
    column_rows = group_count * row_count
    gate_high = gates.astype(jnp.bfloat16)
    gate_low = (gates - gate_high.astype(jnp.float32)).astype(jnp.bfloat16)
    meta = jnp.concatenate([ids.astype(jnp.bfloat16), gate_high, gate_low], axis=1)
    meta = jnp.pad(meta, ((0, 0), (0, 128 - meta.shape[1])))
    packed = lax.all_gather(jnp.concatenate([tokens, meta], axis=1), "grp", axis=0, tiled=True)
    all_tokens = packed[:, :feature]
    all_ids = packed[:, feature : feature + TOPK].astype(jnp.int32)
    all_gates = packed[:, feature + TOPK : feature + 2 * TOPK].astype(jnp.float32) + packed[
        :, feature + 2 * TOPK : feature + 3 * TOPK
    ].astype(jnp.float32)
    my_group = lax.axis_index("grp")
    local = all_ids - pair_count * my_group
    experts = jnp.arange(pair_count, dtype=jnp.int32)
    pick_hot = (local[:, :, None] == experts[None, None, :]).astype(jnp.int32)
    token_hot = jnp.sum(pick_hot, axis=1)
    gate_of = jnp.sum(all_gates[:, :, None] * pick_hot.astype(jnp.float32), axis=1)
    blocks = token_hot.reshape(group_count, row_count, pair_count)
    earlier = (jnp.cumsum(blocks, axis=1) - blocks).reshape(column_rows, pair_count)
    source = jnp.arange(column_rows, dtype=jnp.int32)[:, None] // row_count
    slot_id = experts[None, :] * expert_slots + source * CAP + earlier
    slot_id = jnp.where(token_hot > 0, slot_id, slot_count)
    slots = jnp.arange(slot_count, dtype=jnp.int32)
    match = slot_id[:, :, None] == slots[None, None, :]
    dispatch = jnp.any(match, axis=1).T.astype(jnp.bfloat16)
    combine = jnp.sum(jnp.where(match, gate_of[:, :, None], 0.0), axis=1)
    outgoing = jnp.dot(dispatch, all_tokens, preferred_element_type=jnp.float32).astype(
        jnp.bfloat16
    )
    doubled = jnp.repeat(outgoing.reshape(pair_count, expert_slots, feature), 2, axis=0)
    arriving = lax.all_to_all(doubled, "ep", split_axis=0, concat_axis=0, tiled=True)
    partials = expert_partial(
        arriving.reshape(peer_count * expert_slots, feature), w_gate, w_up, w_down
    ).astype(jnp.bfloat16)
    returned = lax.all_to_all(
        partials.reshape(peer_count, expert_slots, feature),
        "ep",
        split_axis=0,
        concat_axis=0,
        tiled=True,
    )
    expert_out = (
        returned.reshape(pair_count, 2, expert_slots, feature)
        .astype(jnp.float32)
        .sum(axis=1)
        .astype(jnp.bfloat16)
        .reshape(slot_count, feature)
    )
    column_mixed = jnp.dot(
        combine,
        expert_out.astype(jnp.float32),
        precision=lax.Precision.HIGHEST,
        preferred_element_type=jnp.float32,
    )
    mixed = lax.psum_scatter(
        column_mixed.astype(jnp.bfloat16), "grp", scatter_dimension=0, tiled=True
    )
    return (context, mixed)


def solution(mesh):
    in_specs = (
        P(("grp", "ep"), None, None),
        P(("grp", "ep"), None, None),
        P(("grp", "ep")),
        P(("grp", "ep")),
        P(("grp", "ep"), None),
        P(("grp", "ep"), None),
        P(("grp", "ep"), None),
        P(("grp", "ep"), None, None),
        P(("grp", "ep"), None, None),
        P(("grp", "ep"), None, None),
    )
    out_specs = (P(("grp", "ep"), None, None), P(("grp", "ep"), None))
    return jax.shard_map(
        per_device, mesh=mesh, in_specs=in_specs, out_specs=out_specs, check_vma=False
    )
```

profile of v0, /device:TPU:6, one launch (start us, length us, event | category | flops | bytes accessed | tf_op | source)
XLA Modules:
  0.0 250.5 jit_solution(11067031756763123263)
XLA Ops:
  7.2 0.8 copy.35
  8.0 0.8 copy.34
  8.9 1.6 pad_maximum_fusion
  10.5 42.6 %all-gather.2.cloned.1.call-done = bf16[256,3712]{1,0:T(8,128)(2,1)} async-done(((bf16[16,3712]{1,0:T(8,128)(2,1)}), bf16[256,3712]{1,0:T(8,128)(2,1)}) %all-gather.2.cloned.1.call-update) | async-done | bytes 1900560 | tf_op jit(solution)/shard_map/all_gather | solution.py:52
  53.1 1.1 fusion.35
  54.4 0.1 copy.38
  54.5 0.7 fusion.37
  55.5 0.1 copy.40
  55.6 0.7 fusion.6
  56.3 2.2 convolution_convert_fusion.2
  58.5 0.4 broadcast_in_dim.46
  58.9 50.4 %all_to_all.10 = bf16[16,32,3584]{2,1,0:T(8,128)(2,1)S(1)} all-to-all(bf16[16,32,3584]{2,1,0:T(8,128)(2,1)S(1)} %bitcast.38), channel_id=1, replica_groups=mesh['grp'=16,'ep'=16] {'ep'}, dimensions={0} | all-to-all | bytes 7340032 | tf_op jit(solution)/shard_map/all_to_all | solution.py:77
  109.3 1.8 copy-done.1
  111.1 2.0 fusion.4
  113.2 10.0 %convolution_convert_fusion = bf16[512,3584]{1,0:T(8,128)(2,1)} fusion(bf16[1,512,3584]{2,1,0:T(8,128)(2,1)} %param.19, bf16[512,3584]{1,0:T(8,128)(2,1)} %bitcast.43, bf16[1,3584,512]{2,1,0:T(8,128)(2,1)} %param.18, f32[512,512]{1,0:T(8,128)S(1)} %fusion.4), kind=kOutput, calls=%fused_computation.1 | convolution fusion | flops 3761504256 | bytes 15728640 | tf_op jit(solution)/shard_map/dot_general | solution.py:35
  123.2 7.0 %all-to-all-start.1 = ((bf16[16,32,3584]{2,1,0:T(8,128)(2,1)}), bf16[16,32,3584]{2,1,0:T(8,128)(2,1)}, u32[]{:S(2)}, u32[]{:S(2)}) async-start(bf16[16,32,3584]{2,1,0:T(8,128)(2,1)} %bitcast.41), calls=%async_computation.1 | async-start | bytes 7340032 | tf_op jit(solution)/shard_map/all_to_all | solution.py:81
  130.6 1.5 select_reduce_fusion
  132.1 48.8 %all-to-all-done.1 = bf16[16,32,3584]{2,1,0:T(8,128)(2,1)} async-done(((bf16[16,32,3584]{2,1,0:T(8,128)(2,1)}), bf16[16,32,3584]{2,1,0:T(8,128)(2,1)}, u32[]{:S(2)}, u32[]{:S(2)}) %all-to-all-start.1) | async-done | bytes 3670048 | tf_op jit(solution)/shard_map/all_to_all | solution.py:81
  180.9 2.8 %bitcast_reduce_fusion = bf16[8,32,3584]{2,1,0:T(8,128)(2,1)S(1)} fusion(bf16[16,32,3584]{2,1,0:T(8,128)(2,1)} %all-to-all-done.1), kind=kLoop, calls=%fused_computation.4 | loop fusion | flops 917504 | bytes 5505024 | tf_op jit(solution)/shard_map/reduce_sum | solution.py:91
  183.7 2.9 %convolution_convert_fusion.1 = bf16[256,3584]{1,0:T(8,128)(2,1)} fusion(f32[256,256]{1,0:T(8,128)S(1)} %select_reduce_fusion, bf16[256,3584]{1,0:T(8,128)(2,1)S(1)} %bitcast.40), kind=kOutput, calls=%fused_computation.2 | convolution fusion | flops 2819489792 | bytes 3932160 | tf_op jit(solution)/shard_map/dot_general | solution.py:95
  187.3 0.3 fusion.15
  187.7 0.2 fusion.36
  187.9 1.3 fusion.18
  189.2 54.5 %reduce-scatter.2.cloned.1.call-done = bf16[16,3584]{1,0:T(8,128)(2,1)} async-done(((bf16[256,3584]{1,0:T(8,128)(2,1)}), bf16[16,3584]{1,0:T(8,128)(2,1)}) %reduce-scatter.2.cloned.1.call-update) | async-done | bytes 114704 | tf_op jit(solution)/shard_map/reduce_scatter | solution.py:101
  (31 shorter events, 1.0 us)
Async XLA Ops:
  7.2 180.2 %copy-start = (bf16[4,64,576]{2,1,0:T(8,128)(2,1)S(1)}, bf16[4,64,576]{2,1,0:T(8,128)(2,1)}, u32[]{:S(2)}) copy-start(bf16[4,64,576]{2,1,0:T(8,128)(2,1)} %param.10) | copy-start | bytes 884740
  7.2 45.9 %all-gather.2.cloned.1.call-start = ((), (), s32[]{:S(2)}) async-start(), calls=%async_computation.3 | async-start | bytes 2019328 | tf_op jit(solution)/shard_map/all_gather | solution.py:52
  58.9 52.2 %copy-start.4 = (bf16[1,3584,512]{2,1,0:T(8,128)(2,1)S(1)}, bf16[1,3584,512]{2,1,0:T(8,128)(2,1)}, u32[]{:S(2)}) copy-start(bf16[1,3584,512]{2,1,0:T(8,128)(2,1)} %param.17) | copy-start | bytes 11010052
  109.3 1.8 copy-start.1
  123.2 57.6 %all-to-all-start.1 = ((bf16[16,32,3584]{2,1,0:T(8,128)(2,1)}), bf16[16,32,3584]{2,1,0:T(8,128)(2,1)}, u32[]{:S(2)}, u32[]{:S(2)}) async-start(bf16[16,32,3584]{2,1,0:T(8,128)(2,1)} %bitcast.41), calls=%async_computation.1 | async-start | bytes 7340032 | tf_op jit(solution)/shard_map/all_to_all | solution.py:81
  130.2 113.5 %reduce-scatter.2.cloned.1.call-start = ((), (), s32[]{:S(2)}) async-start(), calls=%async_computation.4 | async-start | bytes 1949696 | tf_op jit(solution)/shard_map/reduce_scatter | solution.py:101
  183.7 3.7 %copy-start.2 = (bf16[4,256,576]{1,2,0:T(8,128)(2,1)S(1)}, bf16[4,256,576]{1,2,0:T(8,128)(2,1)}, u32[]{:S(2)}) copy-start(bf16[4,256,576]{1,2,0:T(8,128)(2,1)} %param.11) | copy-start | bytes 3538948
  183.7 3.7 %copy-start.3 = (s32[4]{0:T(128)S(1)}, s32[4]{0:T(128)}, u32[]{:S(2)}) copy-start(s32[4]{0:T(128)} %param.12) | copy-start | bytes 52
Sparse Core Ops, SparseCore 0:
  10.6 42.4 all-gather.1
  186.8 56.8 reduce-scatter.1
where the time goes:
time: 251 us
  waiting for transfers between devices  146 us (58%)
  blocking collectives  50.4 us (20%)
  matrix products  18.8 us (7%)
  between operations  14.9 us (6%)
  other arithmetic  7.73 us (3%)
  starting transfers between devices  7.05 us (3%)
  local copies, waits for them, and re-layouts  5.71 us (2%)
    reduce_scatter x1, waiting for transfers between devices, per_device(): lax.psum_scatter(column_mixed.astype(jnp.bfloat16), 'grp', scatter_dimens...  54.5 us
    all_to_all x1, blocking collectives, per_device(): lax.all_to_all(doubled, 'ep', split_axis=0, concat_axis=0, tiled=True)  50.4 us
    all_to_all x1, waiting for transfers between devices, per_device(): lax.all_to_all(partials.reshape(peer_count, expert_slots, feature), 'ep',...  48.8 us
    all_gather x1, waiting for transfers between devices, per_device(): lax.all_gather(jnp.concatenate([tokens, meta], axis=1), 'grp', axis=0, ti...  42.6 us
    dot_general x1, matrix products, expert_partial(): return jnp.dot(hidden, w_down[0], preferred_element_type=jnp.float32)  10 us
    all_to_all x1, starting transfers between devices, per_device(): lax.all_to_all(partials.reshape(peer_count, expert_slots, feature), 'ep',...  6.97 us
  transfers between devices with their start and end apart: 3, of which 3 were waited for; matrix products, arithmetic and copies ran while one was open for 1% of the time, Pallas kernels for 0%

commit v1 on v0

--- a/solution.py
+++ b/solution.py
@@ -8,6 +8,19 @@
 CAP = 2
 score_scale = 192.0 ** (-0.5)
 neg_large = -1e30
+
+
+def collect(value, axis, dim):
+    ways = lax.axis_size(axis)
+    up = [(d, (d + 1) % ways) for d in range(ways)]
+    down = [(d, (d - 1) % ways) for d in range(ways)]
+    earlier, later = ([value], [value])
+    for _ in range(ways // 2):
+        earlier.append(lax.ppermute(earlier[-1], axis, up))
+    for _ in range((ways - 1) // 2):
+        later.append(lax.ppermute(later[-1], axis, down))
+    line = jnp.concatenate([*earlier[::-1], *later[1:]], axis=dim)
+    return jnp.roll(line, (lax.axis_index(axis) - ways // 2) * value.shape[dim], axis=dim)
 
 
 def attend(queries, cache, lengths, live_count):
@@ -49,7 +62,7 @@
     gate_low = (gates - gate_high.astype(jnp.float32)).astype(jnp.bfloat16)
     meta = jnp.concatenate([ids.astype(jnp.bfloat16), gate_high, gate_low], axis=1)
     meta = jnp.pad(meta, ((0, 0), (0, 128 - meta.shape[1])))
-    packed = lax.all_gather(jnp.concatenate([tokens, meta], axis=1), "grp", axis=0, tiled=True)
+    packed = collect(jnp.concatenate([tokens, meta], axis=1), "grp", 0)
     all_tokens = packed[:, :feature]
     all_ids = packed[:, feature : feature + TOPK].astype(jnp.int32)
     all_gates = packed[:, feature + TOPK : feature + 2 * TOPK].astype(jnp.float32) + packed[

time: 251 us -> 312 us (1.24); the launches traced: 251 us -> 308 us
  local copies, waits for them, and re-layouts: 5.71 us -> 60.8 us
  starting transfers between devices: 7.05 us -> 31.1 us
  waiting for transfers between devices: 146 us -> 127 us
  blocking collectives: 50.4 us -> 46.5 us
    all_gather x1 -> x0, waiting for transfers between devices: 42.6 us -> none  [per_device(): lax.all_gather(jnp.concatenate([tokens, meta], axis=1), 'grp', axis=0, ti...]
    concatenate x0 -> x2, local copies, waits for them, and re-layouts: none -> 31 us  [the longest x1 30.5 us: collect(): jnp.roll(line, (lax.axis_index(axis) - ways // 2) * value.shape[dim], axi...]
    ppermute x0 -> x15, local copies, waits for them, and re-layouts: none -> 25.3 us  [the longest x8 13.3 us: collect(): earlier.append(lax.ppermute(earlier[-1], axis, up))]
    ppermute x0 -> x15, starting transfers between devices: none -> 23.2 us  [the longest x7 23.2 us: collect(): later.append(lax.ppermute(later[-1], axis, down))]
    reduce_scatter x1, waiting for transfers between devices: 54.5 us -> 72.1 us  [per_device(): lax.psum_scatter(column_mixed.astype(jnp.bfloat16), 'grp', scatter_dimens...]
    ppermute x0 -> x15, waiting for transfers between devices: none -> 17.5 us  [the longest x8 17.5 us: collect(): earlier.append(lax.ppermute(earlier[-1], axis, up))]
    all_to_all x1, waiting for transfers between devices: 48.8 us -> 36.9 us  [per_device(): lax.all_to_all(partials.reshape(peer_count, expert_slots, feature), 'ep',...]
    all_to_all x1, blocking collectives: 50.4 us -> 46.5 us  [per_device(): lax.all_to_all(doubled, 'ep', split_axis=0, concat_axis=0, tiled=True)]
  transfers between devices with their start and end apart: 3 -> 17, of which waited for: 3 -> 9; matrix products, arithmetic and copies ran while one was open for 1% -> 9% of each run, Pallas kernels for 0% -> 0%
where the time goes in v1:
time: 312 us; the launch traced here: 308 us
  waiting for transfers between devices  127 us (41%)
  local copies, waits for them, and re-layouts  60.8 us (19%)
  blocking collectives  46.5 us (15%)
  starting transfers between devices  31.1 us (10%)
  matrix products  19.7 us (6%)
  between operations  15 us (5%)
  other arithmetic  8.61 us (3%)
    reduce_scatter x1, waiting for transfers between devices, per_device(): lax.psum_scatter(column_mixed.astype(jnp.bfloat16), 'grp', scatter_dimens...  72.1 us
    all_to_all x1, blocking collectives, per_device(): lax.all_to_all(doubled, 'ep', split_axis=0, concat_axis=0, tiled=True)  46.5 us
    all_to_all x1, waiting for transfers between devices, per_device(): lax.all_to_all(partials.reshape(peer_count, expert_slots, feature), 'ep',...  36.9 us
    concatenate x1, local copies, waits for them, and re-layouts, collect(): jnp.roll(line, (lax.axis_index(axis) - ways // 2) * value.shape[dim], axi...  30.5 us
    ppermute x7, starting transfers between devices, collect(): later.append(lax.ppermute(later[-1], axis, down))  23.2 us
    ppermute x8, waiting for transfers between devices, collect(): earlier.append(lax.ppermute(earlier[-1], axis, up))  17.5 us
    ppermute x8, local copies, waits for them, and re-layouts, collect(): earlier.append(lax.ppermute(earlier[-1], axis, up))  13.3 us
    ppermute x7, local copies, waits for them, and re-layouts, collect(): later.append(lax.ppermute(later[-1], axis, down))  11.9 us
  transfers between devices with their start and end apart: 17, of which 9 were waited for; matrix products, arithmetic and copies ran while one was open for 9% of the time, Pallas kernels for 0%

profile of v1, /device:TPU:6, one launch (start us, length us, event | category | flops | bytes accessed | tf_op | source)
XLA Modules:
  0.0 308.2 jit_solution(10292522962695799508)
XLA Ops:
  9.8 5.3 %collective-permute-start.8 = (bf16[16,3712]{1,0:T(8,128)(2,1)S(1)}, bf16[16,3712]{1,0:T(8,128)(2,1)S(1)}, u32[]{:S(2)}, u32[]{:S(2)}) collective-permute-start(bf16[16,3712]{1,0:T(8,128)(2,1)S(1)} %pad_maximum_fusion), channel_id=1, source_target_pairs={{0,240},{16,0},{32,16},{48,32},{64,48},{80,64},{96,80},{112,96},{1... | collective-permute-start | bytes 356360 | tf_op jit(solution)/shard_map/ppermute | solution.py:21
  15.1 2.5 collective-permute-done
  17.6 3.0 collective-permute-start.9
  20.5 2.5 collective-permute-done.1
  23.0 3.0 collective-permute-start.10
  26.0 2.5 collective-permute-done.2
  28.5 3.0 collective-permute-start.11
  31.5 2.5 collective-permute-done.3
  34.0 3.0 collective-permute-start.12
  37.0 2.5 collective-permute-done.4
  39.5 3.0 collective-permute-start.13
  42.4 2.5 collective-permute-done.5
  45.0 3.1 collective-permute-start.14
  48.0 2.5 collective-permute-done.6
  65.4 2.2 copy.39
  76.4 30.5 %concatenate.14 = bf16[512,3712]{0,1:T(8,128)(2,1)} concatenate(bf16[16,3712]{0,1:T(8,128)(2,1)} %copy.37, bf16[16,3712]{0,1:T(8,128)(2,1)} %copy.38, bf16[16,3712]{0,1:T(8,128)(2,1)} %copy.39, bf16[16,3712]{0,1:T(8,128)(2,1)} %copy.40, bf16[16,3712]{0,1:T(8,128)(2,1)} %copy.41, bf16[16,3712]{0,1:T(8,128)(2,1)} %copy.42, bf16[16,3712]{0,1:T(8,128)(2,1)} %copy.43, ...), dimensions={0} | concatenate | bytes 7602176 | tf_op jit(solution)/shard_map/jit(_roll_dynamic)/concatenate | solution.py:23
  109.7 3.0 convolution_convert_fusion.1
  113.2 46.5 %all_to_all.10 = bf16[16,32,3584]{2,1,0:T(8,128)(2,1)S(1)} all-to-all(bf16[16,32,3584]{2,1,0:T(8,128)(2,1)S(1)} %bitcast.37), channel_id=1, replica_groups=mesh['grp'=16,'ep'=16] {'ep'}, dimensions={0} | all-to-all | bytes 7340032 | tf_op jit(solution)/shard_map/all_to_all | solution.py:90
  163.6 10.1 %convolution_convert_fusion = bf16[512,3584]{1,0:T(8,128)(2,1)} fusion(bf16[1,512,3584]{2,1,0:T(8,128)(2,1)} %param.19, bf16[512,3584]{1,0:T(8,128)(2,1)} %bitcast.42, bf16[1,3584,512]{2,1,0:T(8,128)(2,1)} %param.18, f32[512,512]{1,0:T(8,128)S(1)} %fusion.4), kind=kOutput, calls=%fused_computation.1 | convolution fusion | flops 3761504256 | bytes 15728640 | tf_op jit(solution)/shard_map/dot_general | solution.py:48
  173.7 7.6 %all-to-all-start.1 = ((bf16[16,32,3584]{2,1,0:T(8,128)(2,1)}), bf16[16,32,3584]{2,1,0:T(8,128)(2,1)}, u32[]{:S(2)}, u32[]{:S(2)}) async-start(bf16[16,32,3584]{2,1,0:T(8,128)(2,1)} %bitcast.40), calls=%async_computation.1 | async-start | bytes 7340032 | tf_op jit(solution)/shard_map/all_to_all | solution.py:94
  184.0 36.9 %all-to-all-done.1 = bf16[16,32,3584]{2,1,0:T(8,128)(2,1)} async-done(((bf16[16,32,3584]{2,1,0:T(8,128)(2,1)}), bf16[16,32,3584]{2,1,0:T(8,128)(2,1)}, u32[]{:S(2)}, u32[]{:S(2)}) %all-to-all-start.1) | async-done | bytes 3670048 | tf_op jit(solution)/shard_map/all_to_all | solution.py:94
  220.9 2.8 bitcast_reduce_fusion
  223.8 2.9 convolution_convert_fusion.2
  229.3 72.1 %reduce-scatter.2.cloned.1.call-done = bf16[16,3584]{1,0:T(8,128)(2,1)} async-done(((bf16[256,3584]{1,0:T(8,128)(2,1)}), bf16[16,3584]{1,0:T(8,128)(2,1)}) %reduce-scatter.2.cloned.1.call-update) | async-done | bytes 114704 | tf_op jit(solution)/shard_map/reduce_scatter | solution.py:114
  (91 shorter events, 37.8 us)
Async XLA Ops:
  7.2 220.2 %copy-start = (bf16[4,64,576]{2,1,0:T(8,128)(2,1)S(1)}, bf16[4,64,576]{2,1,0:T(8,128)(2,1)}, u32[]{:S(2)}) copy-start(bf16[4,64,576]{2,1,0:T(8,128)(2,1)} %param.10) | copy-start | bytes 884740
  9.7 7.8 %collective-permute-start = (bf16[16,3712]{1,0:T(8,128)(2,1)S(1)}, bf16[16,3712]{1,0:T(8,128)(2,1)S(1)}, u32[]{:S(2)}, u32[]{:S(2)}) collective-permute-start(bf16[16,3712]{1,0:T(8,128)(2,1)S(1)} %pad_maximum_fusion), channel_id=1, source_target_pairs={{0,16},{16,32},{32,48},{48,64},{64,80},{80,96},{96,112},{112,128},... | collective-permute-start | bytes 356360 | tf_op jit(solution)/shard_map/ppermute | solution.py:19
  9.8 7.8 %collective-permute-start.8 = (bf16[16,3712]{1,0:T(8,128)(2,1)S(1)}, bf16[16,3712]{1,0:T(8,128)(2,1)S(1)}, u32[]{:S(2)}, u32[]{:S(2)}) collective-permute-start(bf16[16,3712]{1,0:T(8,128)(2,1)S(1)} %pad_maximum_fusion), channel_id=1, source_target_pairs={{0,240},{16,0},{32,16},{48,32},{64,48},{80,64},{96,80},{112,96},{1... | collective-permute-start | bytes 356360 | tf_op jit(solution)/shard_map/ppermute | solution.py:21
  17.6 5.5 %collective-permute-start.1 = (bf16[16,3712]{1,0:T(8,128)(2,1)S(1)}, bf16[16,3712]{1,0:T(8,128)(2,1)S(1)}, u32[]{:S(2)}, u32[]{:S(2)}) collective-permute-start(bf16[16,3712]{1,0:T(8,128)(2,1)S(1)} %collective-permute-done), channel_id=1, source_target_pairs={{0,16},{16,32},{32,48},{48,64},{64,80},{80,96},{96,112},{112,128},... | collective-permute-start | bytes 356360 | tf_op jit(solution)/shard_map/ppermute | solution.py:19
  17.6 5.5 %collective-permute-start.9 = (bf16[16,3712]{1,0:T(8,128)(2,1)S(1)}, bf16[16,3712]{1,0:T(8,128)(2,1)S(1)}, u32[]{:S(2)}, u32[]{:S(2)}) collective-permute-start(bf16[16,3712]{1,0:T(8,128)(2,1)S(1)} %collective-permute-done.8), channel_id=1, source_target_pairs={{0,240},{16,0},{32,16},{48,32},{64,48},{80,64},{96,80},{112,96},{1... | collective-permute-start | bytes 356360 | tf_op jit(solution)/shard_map/ppermute | solution.py:21
  23.0 5.5 %collective-permute-start.2 = (bf16[16,3712]{1,0:T(8,128)(2,1)S(1)}, bf16[16,3712]{1,0:T(8,128)(2,1)S(1)}, u32[]{:S(2)}, u32[]{:S(2)}) collective-permute-start(bf16[16,3712]{1,0:T(8,128)(2,1)S(1)} %collective-permute-done.1), channel_id=1, source_target_pairs={{0,16},{16,32},{32,48},{48,64},{64,80},{80,96},{96,112},{112,128},... | collective-permute-start | bytes 356360 | tf_op jit(solution)/shard_map/ppermute | solution.py:19
  23.0 5.5 %collective-permute-start.10 = (bf16[16,3712]{1,0:T(8,128)(2,1)S(1)}, bf16[16,3712]{1,0:T(8,128)(2,1)S(1)}, u32[]{:S(2)}, u32[]{:S(2)}) collective-permute-start(bf16[16,3712]{1,0:T(8,128)(2,1)S(1)} %collective-permute-done.9), channel_id=1, source_target_pairs={{0,240},{16,0},{32,16},{48,32},{64,48},{80,64},{96,80},{112,96},{1... | collective-permute-start | bytes 356360 | tf_op jit(solution)/shard_map/ppermute | solution.py:21
  28.5 22.5 %copy-start.3 = (bf16[16,3712]{1,0:T(8,128)(2,1)}, bf16[16,3712]{1,0:T(8,128)(2,1)S(1)}, u32[]{:S(2)}) copy-start(bf16[16,3712]{1,0:T(8,128)(2,1)S(1)} %collective-permute-done.2) | copy-start | bytes 356356
  28.5 5.5 %collective-permute-start.3 = (bf16[16,3712]{1,0:T(8,128)(2,1)S(1)}, bf16[16,3712]{1,0:T(8,128)(2,1)S(1)}, u32[]{:S(2)}, u32[]{:S(2)}) collective-permute-start(bf16[16,3712]{1,0:T(8,128)(2,1)S(1)} %collective-permute-done.2), channel_id=1, source_target_pairs={{0,16},{16,32},{32,48},{48,64},{64,80},{80,96},{96,112},{112,128},... | collective-permute-start | bytes 356360 | tf_op jit(solution)/shard_map/ppermute | solution.py:19
  28.5 22.5 %copy-start.4 = (bf16[16,3712]{1,0:T(8,128)(2,1)}, bf16[16,3712]{1,0:T(8,128)(2,1)S(1)}, u32[]{:S(2)}) copy-start(bf16[16,3712]{1,0:T(8,128)(2,1)S(1)} %collective-permute-done.10) | copy-start | bytes 356356
  28.5 5.5 %collective-permute-start.11 = (bf16[16,3712]{1,0:T(8,128)(2,1)S(1)}, bf16[16,3712]{1,0:T(8,128)(2,1)S(1)}, u32[]{:S(2)}, u32[]{:S(2)}) collective-permute-start(bf16[16,3712]{1,0:T(8,128)(2,1)S(1)} %collective-permute-done.10), channel_id=1, source_target_pairs={{0,240},{16,0},{32,16},{48,32},{64,48},{80,64},{96,80},{112,96},{1... | collective-permute-start | bytes 356360 | tf_op jit(solution)/shard_map/ppermute | solution.py:21
  34.0 17.1 %copy-start.5 = (bf16[16,3712]{1,0:T(8,128)(2,1)}, bf16[16,3712]{1,0:T(8,128)(2,1)S(1)}, u32[]{:S(2)}) copy-start(bf16[16,3712]{1,0:T(8,128)(2,1)S(1)} %collective-permute-done.3) | copy-start | bytes 356356
  34.0 5.5 %collective-permute-start.4 = (bf16[16,3712]{1,0:T(8,128)(2,1)S(1)}, bf16[16,3712]{1,0:T(8,128)(2,1)S(1)}, u32[]{:S(2)}, u32[]{:S(2)}) collective-permute-start(bf16[16,3712]{1,0:T(8,128)(2,1)S(1)} %collective-permute-done.3), channel_id=1, source_target_pairs={{0,16},{16,32},{32,48},{48,64},{64,80},{80,96},{96,112},{112,128},... | collective-permute-start | bytes 356360 | tf_op jit(solution)/shard_map/ppermute | solution.py:19
  34.0 17.0 %copy-start.7 = (bf16[16,3712]{1,0:T(8,128)(2,1)}, bf16[16,3712]{1,0:T(8,128)(2,1)S(1)}, u32[]{:S(2)}) copy-start(bf16[16,3712]{1,0:T(8,128)(2,1)S(1)} %collective-permute-done.11) | copy-start | bytes 356356
  34.0 5.5 %collective-permute-start.12 = (bf16[16,3712]{1,0:T(8,128)(2,1)S(1)}, bf16[16,3712]{1,0:T(8,128)(2,1)S(1)}, u32[]{:S(2)}, u32[]{:S(2)}) collective-permute-start(bf16[16,3712]{1,0:T(8,128)(2,1)S(1)} %collective-permute-done.11), channel_id=1, source_target_pairs={{0,240},{16,0},{32,16},{48,32},{64,48},{80,64},{96,80},{112,96},{1... | collective-permute-start | bytes 356360 | tf_op jit(solution)/shard_map/ppermute | solution.py:21
  39.5 11.6 %copy-start.9 = (bf16[16,3712]{1,0:T(8,128)(2,1)}, bf16[16,3712]{1,0:T(8,128)(2,1)S(1)}, u32[]{:S(2)}) copy-start(bf16[16,3712]{1,0:T(8,128)(2,1)S(1)} %collective-permute-done.4) | copy-start | bytes 356356
  39.5 5.5 %collective-permute-start.5 = (bf16[16,3712]{1,0:T(8,128)(2,1)S(1)}, bf16[16,3712]{1,0:T(8,128)(2,1)S(1)}, u32[]{:S(2)}, u32[]{:S(2)}) collective-permute-start(bf16[16,3712]{1,0:T(8,128)(2,1)S(1)} %collective-permute-done.4), channel_id=1, source_target_pairs={{0,16},{16,32},{32,48},{48,64},{64,80},{80,96},{96,112},{112,128},... | collective-permute-start | bytes 356360 | tf_op jit(solution)/shard_map/ppermute | solution.py:19
  39.5 5.5 %collective-permute-start.13 = (bf16[16,3712]{1,0:T(8,128)(2,1)S(1)}, bf16[16,3712]{1,0:T(8,128)(2,1)}, u32[]{:S(2)}, u32[]{:S(2)}) collective-permute-start(bf16[16,3712]{1,0:T(8,128)(2,1)S(1)} %collective-permute-done.12), channel_id=1, source_target_pairs={{0,240},{16,0},{32,16},{48,32},{64,48},{80,64},{96,80},{112,96},{1... | collective-permute-start | bytes 356360 | tf_op jit(solution)/shard_map/ppermute | solution.py:21
  44.9 5.6 %collective-permute-start.6 = (bf16[16,3712]{1,0:T(8,128)(2,1)S(1)}, bf16[16,3712]{1,0:T(8,128)(2,1)}, u32[]{:S(2)}, u32[]{:S(2)}) collective-permute-start(bf16[16,3712]{1,0:T(8,128)(2,1)S(1)} %collective-permute-done.5), channel_id=1, source_target_pairs={{0,16},{16,32},{32,48},{48,64},{64,80},{80,96},{96,112},{112,128},... | collective-permute-start | bytes 356360 | tf_op jit(solution)/shard_map/ppermute | solution.py:19
  45.0 27.0 %collective-permute-start.14 = (bf16[16,3712]{1,0:T(8,128)(2,1)}, bf16[16,3712]{1,0:T(8,128)(2,1)}, u32[]{:S(2)}, u32[]{:S(2)}) collective-permute-start(bf16[16,3712]{1,0:T(8,128)(2,1)} %collective-permute-done.13), channel_id=1, source_target_pairs={{0,240},{16,0},{32,16},{48,32},{64,48},{80,64},{96,80},{112,96},{1... | collective-permute-start | bytes 356360 | tf_op jit(solution)/shard_map/ppermute | solution.py:21
  50.5 23.7 %collective-permute-start.7 = (bf16[16,3712]{1,0:T(8,128)(2,1)}, bf16[16,3712]{1,0:T(8,128)(2,1)}, u32[]{:S(2)}, u32[]{:S(2)}) collective-permute-start(bf16[16,3712]{1,0:T(8,128)(2,1)} %collective-permute-done.6), channel_id=1, source_target_pairs={{0,16},{16,32},{32,48},{48,64},{64,80},{80,96},{96,112},{112,128},... | collective-permute-start | bytes 356360 | tf_op jit(solution)/shard_map/ppermute | solution.py:19
  113.1 48.4 %copy-start.14 = (bf16[1,3584,512]{2,1,0:T(8,128)(2,1)S(1)}, bf16[1,3584,512]{2,1,0:T(8,128)(2,1)}, u32[]{:S(2)}) copy-start(bf16[1,3584,512]{2,1,0:T(8,128)(2,1)} %param.17) | copy-start | bytes 11010052
  173.7 47.2 %all-to-all-start.1 = ((bf16[16,32,3584]{2,1,0:T(8,128)(2,1)}), bf16[16,32,3584]{2,1,0:T(8,128)(2,1)}, u32[]{:S(2)}, u32[]{:S(2)}) async-start(bf16[16,32,3584]{2,1,0:T(8,128)(2,1)} %bitcast.40), calls=%async_computation.1 | async-start | bytes 7340032 | tf_op jit(solution)/shard_map/all_to_all | solution.py:94
  181.3 120.0 %reduce-scatter.2.cloned.1.call-start = ((), (), s32[]{:S(2)}) async-start(), calls=%async_computation.3 | async-start | bytes 1949696 | tf_op jit(solution)/shard_map/reduce_scatter | solution.py:114
  (8 other events, 48.3 us)
Sparse Core Ops, SparseCore 0:
  226.8 74.4 reduce-scatter.1
